TPU v7x, 128 devices: a whole 4x4x4 slice. The times are simulated.
128 devices in a mesh: row: 4 (over x), col: 32 (over y, z, core).
Axes of the slice: x: 4, y: 4, z: 4, core: 2. Of those that a mesh axis runs over, the one named last changes fastest.
Arguments:
- factor: float32 [16384, 16384], P('row', 'col'), may hold values from -1 to 2, as said below
- adjoint: float32 [16384, 16384], P('row', 'col'), may hold values from -6 to 6
Outputs:
- panel_adjoint: float32 [16384, 512], P('row')
Inputs may be any that keep to these rules, and one draw needn't show every extreme that they name: In global order, every diagonal block of factor is lower triangular with diagonal entries from 1 to 2.
All inputs are finite; a program needn't handle non-finite values.
Results may differ from a plain program's by a relative error of at most 0.0003.
Values sent between devices are 32-bit elements; how exact they have to be, the bound alone decides.
A program may use at most 192 MiB of HBM per device.

v0:
```python
import jax
import jax.numpy as jnp
from jax import lax
from jax.sharding import PartitionSpec as P

NB = 256


HIGHEST_PRECISION = lax.Precision.HIGHEST


def from_root(block, axis, holder):
    block = jnp.where(lax.axis_index(axis) == holder, block, jnp.zeros_like(block))
    return lax.psum(block, axis)


def matmul(left_side, right_side):
    return jnp.dot(
        left_side, right_side, precision=HIGHEST_PRECISION, preferred_element_type=jnp.float32
    )


def tmatmul(left_side, right_side):
    return lax.dot_general(
        left_side,
        right_side,
        (((0,), (0,)), ((), ())),
        precision=HIGHEST_PRECISION,
        preferred_element_type=jnp.float32,
    )


def lower_half(matrix):
    dimension = matrix.shape[0]
    positions = jnp.arange(dimension, dtype=jnp.int32)
    weight = jnp.where(
        positions[:, None] > positions[None, :],
        1.0,
        jnp.where(positions[:, None] == positions[None, :], 0.5, 0.0),
    )
    return matrix * weight.astype(matrix.dtype)


def inverse_lower(factor_block):
    dimension = factor_block.shape[0]
    if dimension == 1:
        return 1.0 / factor_block
    half_size = dimension // 2
    upper_inv = inverse_lower(factor_block[:half_size, :half_size])
    lower_inv = inverse_lower(factor_block[half_size:, half_size:])
    corner = -matmul(lower_inv, matmul(factor_block[half_size:, :half_size], upper_inv))
    zero_part = jnp.zeros((half_size, dimension - half_size), factor_block.dtype)
    top_rows = jnp.concatenate([upper_inv, zero_part], 1)
    bottom_rows = jnp.concatenate([corner, lower_inv], 1)
    return jnp.concatenate([top_rows, bottom_rows], 0)


def diagonal_adjoint(factor_block, block_bar, inverse):
    inner_part = lower_half(tmatmul(factor_block, block_bar))
    symmetric = tmatmul(inverse, matmul(inner_part, inverse))
    return lower_half(symmetric + symmetric.T)


def local(factor, adjoint):
    n_rows_grid = lax.axis_size("row")
    n_cols_grid = lax.axis_size("col")
    row_id = lax.axis_index("row")
    col_id = lax.axis_index("col")
    local_rows, local_cols = factor.shape
    stride = n_cols_grid // n_rows_grid
    blocks_across = local_cols // NB
    row_ids = jnp.arange(local_rows, dtype=jnp.int32)
    col_ids = jnp.arange(local_cols, dtype=jnp.int32)
    global_row = (row_ids // NB * n_rows_grid + row_id) * NB + row_ids % NB
    global_col = (col_ids // NB * n_cols_grid + col_id) * NB + col_ids % NB
    trailing = (global_row >= 2 * NB)[:, None]
    keep = (global_row[:, None] >= global_col[None, :]) & (global_col[None, :] >= 2 * NB)
    masked = jnp.where(keep, adjoint, 0.0)
    owned_bar = adjoint[:, :NB]
    owner_terms = [jnp.where(col_id == panel_index, owned_bar, 0.0) for panel_index in range(2)]
    received = []
    for panel_index in range(2):
        received.append(from_root(factor[:, :NB], "col", panel_index))
    first_panel, second_panel = received
    q_first = jnp.where(trailing, first_panel, 0.0)
    q_second = jnp.where(trailing, second_panel, 0.0)
    results = []
    for panel_index, chosen_rows in ((1, q_second), (0, q_first)):
        pick_panel_width = chosen_rows.shape[1]
        pick_blocked = chosen_rows.reshape(blocks_across, stride, NB, pick_panel_width)
        chosen = lax.dynamic_index_in_dim(pick_blocked, col_id // n_rows_grid, 1, False)
        transposed = from_root(
            chosen.reshape(blocks_across * NB, pick_panel_width), "row", col_id % n_rows_grid
        )
        col_part = lax.psum(tmatmul(masked, chosen_rows), "row")
        row_part = matmul(masked, transposed)
        panel_width = row_part.shape[1]
        selector = (
            (jnp.arange(stride, dtype=jnp.int32) == col_id // n_rows_grid)
            & (row_id == col_id % n_rows_grid)
        ).astype(jnp.float32)
        blocked = row_part.reshape(blocks_across, stride, NB, panel_width)
        blocked = blocked + selector[None, :, None, None] * col_part.reshape(
            blocks_across, 1, NB, panel_width
        )
        product = blocked.reshape(local_rows, panel_width)
        results.append(lax.psum(owner_terms[panel_index] - product, "col"))
    y_second, y_first = results
    f_head, s_head, fb_head, sb_head = (
        lax.all_gather(first_panel[:NB], "row", axis=0, tiled=True),
        lax.all_gather(second_panel[:NB], "row", axis=0, tiled=True),
        lax.all_gather(y_first[:NB], "row", axis=0, tiled=True),
        lax.all_gather(y_second[:NB], "row", axis=0, tiled=True),
    )
    l_second = jnp.tril(s_head[NB : 2 * NB])
    inv_second = inverse_lower(l_second)
    g_second = jnp.where(trailing, matmul(y_second, inv_second), 0.0)
    diag_second, cross_term = lax.psum(
        (tmatmul(g_second, q_second), tmatmul(g_second, q_first)), "row"
    )
    k_second = jnp.tril(sb_head[NB : 2 * NB]) - jnp.tril(diag_second)
    e_second = diagonal_adjoint(l_second, k_second, inv_second)
    l_first = jnp.tril(f_head[:NB])
    inv_first = inverse_lower(l_first)
    link_block = f_head[NB : 2 * NB]
    head_rows = fb_head[NB : 2 * NB] - matmul(e_second + e_second.T, link_block) - cross_term
    second_block = ((global_row >= NB) & (global_row < 2 * NB))[:, None]
    first_block = (global_row < NB)[:, None]
    filler = jnp.zeros((local_rows - NB, NB), jnp.float32)
    padded_head = jnp.concatenate([head_rows, filler], 0)
    residual = jnp.where(
        trailing, y_first - matmul(g_second, link_block), jnp.where(second_block, padded_head, 0.0)
    )
    g_first = matmul(residual, inv_first)
    diag_first = lax.psum(tmatmul(g_first, first_panel), "row")
    k_first = jnp.tril(fb_head[:NB]) - jnp.tril(diag_first)
    e_first = diagonal_adjoint(l_first, k_first, inv_first)
    left_half = jnp.where(first_block, jnp.concatenate([e_first, filler], 0), g_first)
    right_half = jnp.where(second_block, jnp.concatenate([e_second, filler], 0), g_second)
    return jnp.concatenate([left_half, right_half], 1)


def solution(mesh):
    placed = (P("row", "col"), P("row", "col"))
    return jax.shard_map(
        local, mesh=mesh, in_specs=placed, out_specs=P("row", None), check_vma=False
    )
```

profile of v0, /device:TPU:0, one launch (start us, length us, event | category | flops | bytes accessed | tf_op | source)
XLA Modules:
  0.0 1184.4 jit_solution(2952145861262640278)
XLA Ops:
  6.5 6.1 slice_select_fusion.1
  12.9 123.8 %all-reduce.271.cloned.1.call-done = (f32[4096,256]{1,0:T(8,128)}, f32[4096,256]{1,0:T(8,128)}) async-done(((f32[4096,256]{1,0:T(8,128)}, f32[4096,256]{1,0:T(8,128)}), (f32[4096,256]{1,0:T(8,128)}, f32[4096,256]{1,0:T(8,128)})) %all-reduce.271.cloned.1.call-update) | async-done | bytes 8388624 | tf_op jit(solution)/shard_map/psum | solution.py:14
  136.7 1.7 slice.6169
  138.5 1.7 slice.6684
  140.2 6.0 broadcast_select_fusion.1
  146.3 2.5 dynamic-slice_select_fusion
  148.8 19.9 %fusion.4073 = f32[512,256]{1,0:T(8,128)} fusion(f32[4096,256]{1,0:T(8,128)} %get-tuple-element.785, f32[4096,512]{1,0:T(8,128)} %param.3, s32[512]{0:T(512)S(1)} %fusion.1686, s32[4096]{0:T(1024)S(1)} %fusion.309, pred[512]{0:T(512)(128)(4,1)S(1)} %broadcast_compare_fusion.2), kind=kOutput, calls=%fused_computation.4626 | convolution fusion | flops 6448742400 | bytes 13126144 | tf_op jit(solution)/shard_map/dot_general | solution.py:24
  168.8 26.5 %fusion.4072 = f32[512,256]{1,0:T(8,128)} fusion(f32[4096,256]{1,0:T(8,128)S(1)} %copy-done.2, f32[4096,512]{1,0:T(8,128)S(1)} %bitcast.553, s32[512]{0:T(512)S(1)} %fusion.1686, s32[4096]{0:T(1024)S(1)} %fusion.309, pred[512]{0:T(512)(128)(4,1)S(1)} %broadcast_compare_fusion.2), kind=kOutput, calls=%fused_computation.4625 | convolution fusion | flops 6448742400 | bytes 13126144 | tf_op jit(solution)/shard_map/dot_general | solution.py:24
  195.4 1.0 slice_select_fusion.5
  236.8 0.7 fusion.4090
  247.0 0.7 fusion.4089
  274.9 0.7 fusion.4088
  284.8 0.7 fusion.4087
  287.7 0.7 fusion.4086
  309.6 0.7 fusion.4079
  319.6 0.7 fusion.4077
  324.7 0.7 fusion.4078
  330.2 0.7 fusion.4076
  359.1 0.7 fusion.4075
  359.9 0.7 fusion.4074
  379.7 0.7 fusion.4081
  380.4 0.7 fusion.4082
  381.2 0.7 fusion.4083
  435.0 1.0 slice_select_fusion.3
  436.0 0.7 fusion.4116
  441.5 0.7 fusion.4115
  442.2 0.7 fusion.4114
  452.0 0.7 fusion.4113
  475.9 0.7 fusion.4112
  485.8 0.7 fusion.4111
  513.4 1.1 fusion.4110
  523.9 0.7 fusion.4109
  526.9 0.7 fusion.4108
  548.6 0.7 fusion.4101
  558.6 0.7 fusion.4099
  569.0 0.7 fusion.4098
  597.5 0.8 fusion.4097
  634.9 0.7 fusion.4103
  636.4 0.7 fusion.4105
  639.3 0.7 fusion.4107
  843.6 2.1 bitcast_multiply_fusion.1
  845.7 12.3 %fusion.1 = f32[4096,256]{1,0:T(8,128)} fusion(f32[4096,256]{1,0:T(8,128)S(1)} %get-tuple-element.783, f32[512,256]{1,0:T(8,128)S(1)} %copy-done.9, f32[4096,512]{1,0:T(8,128)} %param.3, pred[]{:T(512)S(6)} %eq.34, s32[512]{0:T(512)S(1)} %fusion.1686, s32[4096]{0:T(1024)S(1)} %fusion.309, pred[512]{0:T(512)(128)(4,1)S(1)} %broadcast_compare_fusion.2), kind=kOutput, calls=%fused_computation.7 | convolution fusion | flops 6451888128 | bytes 21514752 | tf_op jit(solution)/shard_map/dot_general | solution.py:18
  858.0 9.5 fusion.2
  871.7 116.6 %all-reduce.269.cloned.1.call-done = (f32[4096,256]{1,0:T(8,128)}, f32[4096,256]{1,0:T(8,128)}) async-done(((f32[4096,256]{1,0:T(8,128)}, f32[4096,256]{1,0:T(8,128)}), (f32[4096,256]{1,0:T(8,128)}, f32[4096,256]{1,0:T(8,128)})) %all-reduce.269.cloned.1.call-update) | async-done | bytes 8388624 | tf_op jit(solution)/shard_map/psum | solution.py:107
  988.3 6.8 convolution_select_fusion
  995.2 7.5 fusion.4119
  1002.6 7.6 fusion.4118
  1010.8 1.7 slice.7199
  1014.1 1.7 slice.6682
  1016.7 36.1 %all-reduce.273.cloned.1.call-done = (f32[256,256]{1,0:T(8,128)}, f32[256,256]{1,0:T(8,128)}) async-done(((f32[256,256]{1,0:T(8,128)}, f32[256,256]{1,0:T(8,128)}), (f32[256,256]{1,0:T(8,128)}, f32[256,256]{1,0:T(8,128)})) %all-reduce.273.cloned.1.call-update) | async-done | bytes 524304 | tf_op jit(solution)/shard_map/psum | solution.py:118
  1052.8 26.4 %all-gather.11.cloned.1.call-done = f32[1024,256]{1,0:T(8,128)} async-done(((f32[256,256]{1,0:T(8,128)}), f32[1024,256]{1,0:T(8,128)}) %all-gather.11.cloned.1.call-update) | async-done | bytes 1048592 | tf_op jit(solution)/shard_map/all_gather | solution.py:113
  1079.2 1.6 convolution_multiply_fusion.1
  1082.0 23.3 %all-gather.7.cloned.1.call-done = f32[1024,256]{1,0:T(8,128)} async-done(((f32[256,256]{1,0:T(8,128)}), f32[1024,256]{1,0:T(8,128)}) %all-gather.7.cloned.1.call-update) | async-done | bytes 1048592 | tf_op jit(solution)/shard_map/all_gather | solution.py:112
  1105.3 1.4 fusion.3
  1106.7 6.7 fusion
  1113.3 4.0 fusion.4070
  1117.3 2.0 copy-done.1
  1119.4 4.3 fusion.4120
  1123.7 4.0 pad_select_fusion
  1127.7 5.6 copy.8
  1133.3 32.5 %all-reduce.267.cloned.1.call-done = f32[256,256]{1,0:T(8,128)} async-done(((f32[256,256]{1,0:T(8,128)}), f32[256,256]{1,0:T(8,128)}) %all-reduce.267.cloned.1.call-update) | async-done | bytes 262160 | tf_op jit(solution)/shard_map/psum | solution.py:135
  1165.8 1.5 convolution_multiply_fusion
  1168.5 4.3 pad_select_fusion.1
  1172.9 4.7 pad_maximum_fusion
  (923 shorter events, 133.1 us)
Async XLA Ops:
  6.5 130.2 %all-reduce.271.cloned.1.call-start = ((), (), s32[]{:S(2)}) async-start(), calls=%async_computation.6 | async-start | bytes 16777216 | tf_op jit(solution)/shard_map/psum | solution.py:14
  12.7 182.7 %all-gather.5.cloned.1.call-start = ((), (), s32[]{:S(2)}) async-start(), calls=%async_computation | async-start | bytes 1310720 | tf_op jit(solution)/shard_map/all_gather | solution.py:110
  138.4 296.6 %all-gather.9.cloned.1.call-start = ((), (), s32[]{:S(2)}) async-start(), calls=%async_computation.2 | async-start | bytes 1310720 | tf_op jit(solution)/shard_map/all_gather | solution.py:111
  146.2 697.3 %all-reduce.275.cloned.1.call-start = ((), (), s32[]{:S(2)}) async-start(), calls=%async_computation.8 | async-start | bytes 4194304 | tf_op jit(solution)/shard_map/psum | solution.py:95
  146.3 22.5 %slice-start = ((s8[8388608]{0:T(1024)(128)(4,1)}), s8[4194304]{0:T(1024)(128)(4,1)S(1)}, s32[]{:S(2)}) async-start(s8[8388608]{0:T(1024)(128)(4,1)} %bitcast.552), calls=%async_computation.9 | async-start | bytes 8388608
  148.8 19.9 %slice-start.1 = ((s8[8388608]{0:T(1024)(128)(4,1)}), s8[4194304]{0:T(1024)(128)(4,1)S(1)}, s32[]{:S(2)}) async-start(s8[8388608]{0:T(1024)(128)(4,1)} %bitcast.552), calls=%async_computation.10 | async-start | bytes 8388608
  148.8 19.9 %copy-start.2 = (f32[4096,256]{1,0:T(8,128)S(1)}, f32[4096,256]{1,0:T(8,128)}, u32[]{:S(2)}) copy-start(f32[4096,256]{1,0:T(8,128)} %get-tuple-element.786) | copy-start | bytes 12582916
  195.3 793.0 %all-reduce.269.cloned.1.call-start = ((), (), s32[]{:S(2)}) async-start(), calls=%async_computation.5 | async-start | bytes 16777216 | tf_op jit(solution)/shard_map/psum | solution.py:107
  843.6 2.1 copy-start.9
  843.6 14.4 %slice-start.2 = ((s8[8388608]{0:T(1024)(128)(4,1)}), s8[4194304]{0:T(1024)(128)(4,1)S(1)}, s32[]{:S(2)}) async-start(s8[8388608]{0:T(1024)(128)(4,1)} %bitcast.554), calls=%async_computation.11 | async-start | bytes 8388608
  845.7 12.3 %slice-start.3 = ((s8[8388608]{0:T(1024)(128)(4,1)}), s8[4194304]{0:T(1024)(128)(4,1)S(1)}, s32[]{:S(2)}) async-start(s8[8388608]{0:T(1024)(128)(4,1)} %bitcast.554), calls=%async_computation.12 | async-start | bytes 8388608
  845.7 12.3 %copy-start.8 = (f32[512,256]{1,0:T(8,128)S(1)}, f32[512,256]{1,0:T(8,128)}, u32[]{:S(2)}) copy-start(f32[512,256]{1,0:T(8,128)} %get-tuple-element.12) | copy-start | bytes 1572868
  867.5 185.3 %all-reduce.273.cloned.1.call-start = ((), (), s32[]{:S(2)}) async-start(), calls=%async_computation.7 | async-start | bytes 1048576 | tf_op jit(solution)/shard_map/psum | solution.py:118
  988.3 6.8 copy-start.4
  995.1 7.5 copy-start
  995.1 7.5 copy-start.3
  1010.3 68.9 %all-gather.11.cloned.1.call-start = ((), (), s32[]{:S(2)}) async-start(), calls=%async_computation.3 | async-start | bytes 1310720 | tf_op jit(solution)/shard_map/all_gather | solution.py:113
  1012.6 92.7 %all-gather.7.cloned.1.call-start = ((), (), s32[]{:S(2)}) async-start(), calls=%async_computation.1 | async-start | bytes 1310720 | tf_op jit(solution)/shard_map/all_gather | solution.py:112
  1015.8 150.0 %all-reduce.267.cloned.1.call-start = ((), (), s32[]{:S(2)}) async-start(), calls=%async_computation.4 | async-start | bytes 524288 | tf_op jit(solution)/shard_map/psum | solution.py:135
  1016.1 89.1 %copy-start.7 = (f32[1024,256]{1,0:T(8,128)S(1)}, f32[1024,256]{1,0:T(8,128)}, u32[]{:S(2)}) copy-start(f32[1024,256]{1,0:T(8,128)} %all-gather.5.cloned.1.call-done) | copy-start | bytes 3145732
  1052.8 52.5 %copy-start.10 = (f32[256,256]{1,0:T(8,128)S(1)}, f32[256,256]{1,0:T(8,128)}, u32[]{:S(2)}) copy-start(f32[256,256]{1,0:T(8,128)} %get-tuple-element.10) | copy-start | bytes 786436
  1113.3 6.0 copy-start.5
  1117.3 2.0 copy-start.1
  1168.5 4.4 copy-start.6
Sparse Core Ops, SparseCore 0:
  12.8 123.8 all-reduce.270
  138.5 23.2 all-gather.4
  163.6 24.2 all-gather.8
  195.4 58.6 all-reduce.274
  867.6 120.6 all-reduce.268
  1010.4 42.3 all-reduce.272
  1054.6 24.5 all-gather.10
  1080.9 24.2 all-gather.6
  1123.8 41.9 all-reduce.266
where the time goes:
time: 1200 us; the launch traced here: 1180 us
  between operations  515 us (43%)
  waiting for transfers between devices  359 us (30%)
  matrix products  214 us (18%)
  other arithmetic  49.1 us (4%)
  local copies, waits for them, and re-layouts  47.6 us (4%)
    dot_general x516, matrix products, matmul(): jnp.dot(left_side, right_side, precision=HIGHEST_PRECISION, preferred_ele...  144 us
    psum x1, waiting for transfers between devices, from_root(): return lax.psum(block, axis)  124 us
    psum x1, waiting for transfers between devices, local(): results.append(lax.psum(owner_terms[panel_index] - product, 'col'))  117 us
    dot_general x9, matrix products, tmatmul(): lax.dot_general(left_side, right_side, (((0,), (0,)), ((), ())), precisio...  70.1 us
    psum x1, waiting for transfers between devices, local(): lax.psum((tmatmul(g_second, q_second), tmatmul(g_second, q_first)), 'row')  36.1 us
    psum x1, waiting for transfers between devices, local(): diag_first = lax.psum(tmatmul(g_first, first_panel), 'row')  32.5 us
    all_gather x1, waiting for transfers between devices, local(): lax.all_gather(y_second[:NB], 'row', axis=0, tiled=True)  26.4 us
  transfers between devices with their start and end apart: 9, of which 6 were waited for; matrix products, arithmetic and copies ran while one was open for 19% of the time, Pallas kernels for 0%

commit v1 on v0

v1 whole, which is shorter than its diff:
```python
import jax
import jax.numpy as jnp
from jax import lax
from jax.experimental import pallas as pl
from jax.experimental.pallas import tpu as pltpu
from jax.sharding import PartitionSpec as P

NB = 256
HIGHEST = lax.Precision.HIGHEST
HIGH = lax.Precision.HIGH


def dot(a, b, precision=HIGHEST):
    return lax.dot_general(a, b, (((1,), (0,)), ((), ())), precision=precision, preferred_element_type=jnp.float32)


def tdot(a, b, precision=HIGHEST):
    return lax.dot_general(a, b, (((0,), (0,)), ((), ())), precision=precision, preferred_element_type=jnp.float32)


def grid_ids(n):
    return lax.broadcasted_iota(jnp.int32, (n, n), 0), lax.broadcasted_iota(jnp.int32, (n, n), 1)


def lower(x):
    i, j = grid_ids(x.shape[0])
    return jnp.where(i >= j, x, 0.0)


def lower_half(x):
    i, j = grid_ids(x.shape[0])
    return jnp.where(i > j, x, jnp.where(i == j, 0.5 * x, 0.0))


def inverse_lower(mats):
    n = mats[0].shape[0]
    i, j = grid_ids(n)
    found = []
    for m in mats:
        d = jnp.where(i == j, m, 0.0)
        found.append(jnp.where(i == j, 1.0 / jnp.where(i == j, m, 1.0), 0.0))
    k = 1
    while k < n:
        corner = (i // (2 * k) == j // (2 * k)) & (i // k > j // k)
        inner = [dot(jnp.where(corner, m, 0.0), x) for m, x in zip(mats, found)]
        found = [x - dot(x, y) for x, y in zip(found, inner)]
        k *= 2
    return found


MESH = pl.DeviceIdType.MESH
ROWS, HEAD, CHUNK = 4096, 512, 32
STEPS, LAG = 36, 5
DEPTH = ((0, 3, 4, 3, 3, 4, 5, 4, 2, 3, 4, 3, 1, 2, 3, 2), (0, 3, 2, 1, 3, 4, 3, 2, 4, 5, 4, 3, 3, 4, 3, 2),
         (0, 3, 4, 3, 1, 2, 3, 2, 2, 3, 4, 3, 3, 4, 5, 4), (0, 1, 2, 3, 3, 2, 3, 4, 4, 3, 4, 5, 3, 2, 3, 4))
TREE_OF_LINK = ((2, 3, 3, 1, 2, 2, 3, 1, 2, 2, 2, 2, 9, 0, 0, 0), (3, 3, 3, 9, 2, 2, 3, 1, 0, 0, 3, 1, 0, 3, 3, 1),
                (0, 3, 1, 1, 9, 2, 2, 2, 0, 0, 0, 0, 0, 3, 1, 0), (1, 9, 1, 1, 2, 3, 1, 1, 2, 3, 1, 2, 0, 3, 1, 0))
LINKS = ((1, 0), (0, 1), (3, 0), (0, 3))


def place():
    r, c = lax.axis_index("row"), lax.axis_index("col")
    return r, c, c // 8, (c // 2) % 4, c % 2


def at(r, y, z, k):
    return {"row": r, "col": (y * 4 + z) * 2 + k}


def pick(index, table):
    value = jnp.int32(table[0])
    for i, entry in enumerate(table[1:], 1):
        value = jnp.where(index == i, jnp.int32(entry), value)
    return value


def remote(src, dst, send, recv, device):
    return pltpu.make_async_remote_copy(
        src_ref=src, dst_ref=dst, send_sem=send, recv_sem=recv, device_id=device, device_id_type=MESH
    )


def meet(devices):
    barrier = pltpu.get_barrier_semaphore()
    for device in devices:
        pl.semaphore_signal(barrier, inc=1, device_id=device, device_id_type=MESH)
    pl.semaphore_wait(barrier, len(devices))


def broadcast_kernel(f_ref, p_ref, q_ref, send, sib_send, recv, sib_recv, x_send, x_recv, h_send, h_recv, own):
    r, c, y, z, k = place()
    chip = y * 4 + z
    sibling = at(r, y, z, 1 - k)
    nexts = [at(r, (y + dy) % 4, (z + dz) % 4, k) for dy, dz in LINKS]
    xs = [at((r + d) % 4, y, z, k) for d in (1, 3, 2)]
    meet(nexts + [sibling] + xs)
    depth = [pick(chip, row) for row in DEPTH]
    tree = [pick(chip, row) for row in TREE_OF_LINK]
    is_root = chip == 0

    def first_row(s, t):
        u = jnp.where(s < 8, s, s - 4)
        body = ((u % 8) * 2 + t // 2) * NB + (u // 8) * 64 + (t % 2) * CHUNK
        head = ROWS + ((s - 8) * 4 + t) * CHUNK
        return pl.multiple_of(jnp.where((s >= 8) & (s < 12), head, body), CHUNK)

    def pass_on(s, t, src, dst):
        remote(src, dst, sib_send.at[s, t], sib_recv.at[s, t], sibling).start()
        for d in range(4):
            @pl.when(tree[d] == t)
            def _():
                remote(src, dst, send.at[d, s], recv.at[s, t], nexts[d]).start()

    @pl.when(is_root)
    def _():
        pltpu.make_async_copy(f_ref.at[:, pl.ds(0, NB)], p_ref.at[k, pl.ds(0, ROWS), :], own.at[0]).start()
        for head in range(2):
            rows = p_ref.at[k, pl.ds(ROWS + head * NB, NB), :]
            block = f_ref.at[pl.ds(0, NB), pl.ds(0, NB)]

            @pl.when(r == head)
            def _():
                pltpu.make_async_copy(block, rows, own.at[1]).start()
                for i, device in enumerate(xs):
                    remote(block, rows, h_send.at[i], h_recv.at[head], device).start()

        def from_own(s, _):
            for t in range(4):
                rows = p_ref.at[k, pl.ds(first_row(s, t), CHUNK), :]
                pass_on(s, t, rows, rows)

        pltpu.make_async_copy(f_ref.at[:, pl.ds(0, NB)], p_ref.at[k, pl.ds(0, ROWS), :], own.at[0]).wait()
        lax.fori_loop(0, 8, from_own, None)
        for head in range(2):
            rows = p_ref.at[k, pl.ds(ROWS + head * NB, NB), :]

            @pl.when(r == head)
            def _():
                pltpu.make_async_copy(rows, rows, own.at[1]).wait()
                for i, device in enumerate(xs):
                    remote(rows, rows, h_send.at[i], h_recv.at[head], device).wait_send()

            @pl.when(r != head)
            def _():
                remote(rows, rows, h_send.at[0], h_recv.at[head], xs[0]).wait_recv()

        lax.fori_loop(8, STEPS, from_own, None)

    def forward(n, _):
        for t in range(4):
            s = n - LAG * (depth[t] - 1)

            @pl.when((s >= 0) & (s < STEPS))
            def _():
                rows = p_ref.at[k, pl.ds(first_row(s, t), CHUNK), :]
                remote(rows, rows, sib_send.at[s, t], recv.at[s, t], sibling).wait_recv()
                pass_on(s, t, rows, rows)

    m = c // 4
    stops = [8 + LAG * 4, 20 + LAG * 4, 28 + LAG * 4, 36 + LAG * 4]
    for j in range(4):
        @pl.when(jnp.logical_not(is_root))
        def _():
            lax.fori_loop(stops[j - 1] if j else 0, stops[j], forward, None)

        @pl.when(r == c % 4)
        def _():
            for b in range(2):
                row = pl.multiple_of((m + 8 * b) * NB + j * 64, 64)
                s = (j * 8 + 4 * b + m // 2) + (4 if j else 0)
                for half in range(2):
                    t = (m % 2) * 2 + half
                    got = p_ref.at[1 - k, pl.ds(row + half * CHUNK, CHUNK), :]
                    remote(got, got, sib_send.at[s, t], sib_recv.at[s, t], sibling).wait_recv()
                src = p_ref.at[:, pl.ds(row, 64), :]
                dst = q_ref.at[:, pl.ds(b * NB + j * 64, 64), :]
                pltpu.make_async_copy(src, dst, own.at[2 + j * 2 + b]).start()
                for i, device in enumerate(xs):
                    remote(src, dst, x_send.at[j, b, i], x_recv.at[j, b], device).start()

    def finish(s, _):
        for t in range(4):
            row = first_row(s, t)
            mine = p_ref.at[k, pl.ds(row, CHUNK), :]
            other = p_ref.at[1 - k, pl.ds(row, CHUNK), :]
            remote(mine, mine, sib_send.at[s, t], sib_recv.at[s, t], sibling).wait_send()
            u = jnp.where(s < 8, s, s - 4)
            block = (u % 8) * 2 + t // 2
            early = (r == c % 4) & ((s < 8) | (s >= 12)) & (block % 8 == m)

            @pl.when(jnp.logical_not(early))
            def _():
                remote(other, other, sib_send.at[s, t], sib_recv.at[s, t], sibling).wait_recv()
        for d in range(4):
            @pl.when(tree[d] < 4)
            def _():
                rows = p_ref.at[k, pl.ds(0, CHUNK), :]
                remote(rows, rows, send.at[d, s], recv.at[s, 0], nexts[d]).wait_send()

    lax.fori_loop(0, STEPS, finish, None)
    for j in range(4):
        for b in range(2):
            src = p_ref.at[:, pl.ds(0, 64), :]
            dst = q_ref.at[:, pl.ds(b * NB + j * 64, 64), :]

            @pl.when(r == c % 4)
            def _():
                pltpu.make_async_copy(src, dst, own.at[2 + j * 2 + b]).wait()
                for i, device in enumerate(xs):
                    remote(src, dst, x_send.at[j, b, i], x_recv.at[j, b], device).wait_send()

            @pl.when(r != c % 4)
            def _():
                remote(src, dst, x_send.at[j, b, 0], x_recv.at[j, b], xs[0]).wait_recv()


def broadcast(factor):
    dma = pltpu.SemaphoreType.DMA
    anywhere = pl.BlockSpec(memory_space=pl.ANY)
    return pl.pallas_call(
        broadcast_kernel,
        out_shape=(jax.ShapeDtypeStruct((2, ROWS + HEAD, NB), jnp.float32), jax.ShapeDtypeStruct((2, 512, NB), jnp.float32)),
        in_specs=[anywhere],
        out_specs=(pl.BlockSpec(memory_space=pltpu.VMEM),) * 2,
        scratch_shapes=[dma((4, STEPS)), dma((STEPS, 4)), dma((STEPS, 4)), dma((STEPS, 4)), dma((4, 2, 3)), dma((4, 2)),
                        dma((3,)), dma((2,)), dma((10,))],
        compiler_params=pltpu.CompilerParams(collective_id=1, has_side_effects=True, vmem_limit_bytes=40 << 20),
    )(factor)


def split(x):
    high = x.astype(jnp.bfloat16)
    return high, (x - high.astype(jnp.float32)).astype(jnp.bfloat16)


def dot3(a, b, dims):
    def one(x, w):
        return lax.dot_general(x, w, (dims, ((), ())), preferred_element_type=jnp.float32)
    return one(a[0], b[0]) + (one(a[0], b[1]) + one(a[1], b[0]))


def product_kernel(a_ref, p_ref, q_ref, w_ref, col_ref, m_ref, row_acc, qh, ql):
    step = pl.program_id(0)
    r, c = lax.axis_index("row"), lax.axis_index("col")
    block = 4 * step + r
    i, j = grid_ids(NB)

    @pl.when(step == 0)
    def _():
        col_ref[...] = jnp.zeros_like(col_ref)
        m_ref[...] = jnp.zeros_like(m_ref)
        for b in range(2):
            for k in range(2):
                qh[b, :, k * NB:(k + 1) * NB], ql[b, :, k * NB:(k + 1) * NB] = split(q_ref[k, b * NB:(b + 1) * NB, :])
        for head, (hr, hc, lo, side) in enumerate([(0, 0, 768, 0), (1, 0, 512, 0), (1, 1, 512, NB)]):
            @pl.when((r == hr) & (c == hc))
            def _():
                m_ref[lo:lo + NB, side:side + NB] = a_ref[:, :NB]

    row_acc[...] = jnp.zeros_like(row_acc)
    panel = split(jnp.concatenate([p_ref[0], p_ref[1]], 1))
    for b in range(2):
        column = 32 * b + c
        owner = (column < 2)

        @pl.when((block >= column) & (block >= 2))
        def _():
            tile = a_ref[:, b * NB:(b + 1) * NB]
            tile = jnp.where((block > column) | (i >= j), tile, 0.0)
            tile = split(tile)
            col_ref[b] += dot3(tile, panel, ((0,), (0,)))

            @pl.when(jnp.logical_not(owner))
            def _():
                row_acc[...] += dot3(tile, (qh[b], ql[b]), ((1,), (0,)))

    for side in range(2):
        part = slice(side * NB, (side + 1) * NB)
        own = jnp.where(c == side, a_ref[:, :NB], 0.0)
        w_ref[:, part] = own - row_acc[:, part]

    @pl.when(step == pl.num_programs(0) - 1)
    def _():
        for side in range(2):
            @pl.when(c == side)
            def _():
                m_ref[side * NB:(side + 1) * NB, :] = col_ref[0]

        @pl.when(c < 2)
        def _():
            col_ref[0] = jnp.zeros((NB, 512), jnp.float32)

        s = jnp.zeros((512, 512), jnp.float32)
        for b in range(2):
            s += dot3(split(col_ref[b]), (qh[b], ql[b]), ((0,), (0,)))
        m_ref[:512] += -s - s.T


def products(adjoint, p, q):
    return pl.pallas_call(
        product_kernel,
        out_shape=(jax.ShapeDtypeStruct((ROWS, 512), jnp.float32), jax.ShapeDtypeStruct((2, NB, 512), jnp.float32),
                   jax.ShapeDtypeStruct((1024, 512), jnp.float32)),
        grid=(16,),
        in_specs=[pl.BlockSpec((NB, 512), lambda a: (a, 0)), pl.BlockSpec((2, NB, NB), lambda a: (0, a, 0)),
                  pl.BlockSpec((2, 512, NB), lambda a: (0, 0, 0))],
        out_specs=(pl.BlockSpec((NB, 512), lambda a: (a, 0)), pl.BlockSpec((2, NB, 512), lambda a: (0, 0, 0)),
                   pl.BlockSpec((1024, 512), lambda a: (0, 0))),
        scratch_shapes=[pltpu.VMEM((NB, 512), jnp.float32), pltpu.VMEM((2, NB, 512), jnp.bfloat16), pltpu.VMEM((2, NB, 512), jnp.bfloat16)],
        compiler_params=pltpu.CompilerParams(vmem_limit_bytes=40 << 20),
    )(adjoint, p, q)


def reduce_kernel(w_ref, col_ref, m_ref, h_ref, o_ref, top_ref, acc, sib, r1, r2, part, t1, t2, v, col_x, col_p, m_a, m_s, m_x, m_b,
                  m_y, m_c, m_z, m_f, s0, s1, s2, s3, s4, sc, sp, sm, g1, g2, gs):
    r, c, y, z, k = place()
    sibling = at(r, y, z, 1 - k)
    xp = [at((r + d) % 4, y, z, k) for d in (1, 2, 3)]
    yp = [at(r, (y + d) % 4, z, k) for d in (1, 2, 3)]
    zp = [at(r, y, (z + d) % 4, k) for d in (1, 2, 3)]
    own_col = c % 4
    m_id = c // 4
    chip = y * 4 + z
    source = (4 * chip + r) % 32
    barrier = pltpu.get_barrier_semaphore()
    for device in xp + yp + zp + [sibling]:
        pl.semaphore_signal(barrier, inc=1, device_id=device, device_id_type=MESH)
    others = jnp.int32(0)
    targets = [2 * (m_id + 8 * b) + h for b in range(2) for h in range(2)]
    for target in targets:
        others += jnp.where((r == own_col) & (target != c), 1, 0).astype(jnp.int32)

    @pl.when(source != c)
    def _():
        pl.semaphore_signal(barrier, inc=1, device_id={"row": r, "col": source}, device_id_type=MESH)
    pl.semaphore_wait(barrier, 10 + others)

    sent = []

    def send(src, dst, sems, index, device):
        copy = remote(src, dst, sems.at[(0, *index)], sems.at[(1, *index)], device)
        copy.start()
        sent.append(copy)

    def arrive(dst, sems, index):
        remote(dst, dst, sems.at[(0, *index)], sems.at[(1, *index)], sibling).wait_recv()

    first = [z, y]
    second = [y, z]
    first_peers, second_peers = [zp, yp], [yp, zp]

    def w_shard(f, h, i):
        return w_ref.at[:, i, h, 0] if f == 0 else w_ref.at[i, :, h, 1]

    send(m_ref.at[1 - k], m_s, sm, (0, 0), sibling)
    for j in (2, 1, 3, 0):
        for f in range(2):
            i = (first[f] + j) % 4
            send(w_shard(f, 1 - k, i), sib.at[f, i], s0, (f, j), sibling)

    @pl.when(r != own_col)
    def _():
        slot = (own_col - r + 4) % 4 - 1
        remote(col_ref, col_x.at[slot], sc.at[0, 0], sc.at[1, slot], {"row": own_col, "col": c}).start()

    arrive(m_s, sm, (0, 0))
    m_a[...] = m_ref[k] + m_s[...]
    for d in range(3):
        send(m_a.at[(r + d + 1) % 4], m_x.at[d], sm, (1, d), xp[d])

    for j in (2, 1, 3, 0):
        for f in range(2):
            i = (first[f] + j) % 4
            arrive(sib.at[f, i], s0, (f, j))
            acc[f, i] = w_shard(f, k, i)[...] + sib[f, i]
            up, down = first_peers[f][0], first_peers[f][2]
            if j == 2:
                send(acc.at[f, i, pl.ds(0, 2)], r1.at[f, 0], s1, (f, 0), up)
                send(acc.at[f, i, pl.ds(2, 2)], r1.at[f, 1], s1, (f, 1), down)
            if j == 1:
                send(acc.at[f, i, pl.ds(2, 2)], r2.at[f, 0, pl.ds(2, 2)], s2, (f, 0, 1), up)
            if j == 3:
                send(acc.at[f, i, pl.ds(0, 2)], r2.at[f, 1, pl.ds(0, 2)], s2, (f, 1, 0), down)
    for f in range(2):
        up, down = first_peers[f][0], first_peers[f][2]
        i = (first[f] + 1) % 4
        arrive(r1.at[f, 0], s1, (f, 0))
        acc[f, i, 0:2] = acc[f, i, 0:2] + r1[f, 0]
        send(acc.at[f, i, pl.ds(0, 2)], r2.at[f, 0, pl.ds(0, 2)], s2, (f, 0, 0), up)
        i = (first[f] + 3) % 4
        arrive(r1.at[f, 1], s1, (f, 1))
        acc[f, i, 2:4] = acc[f, i, 2:4] + r1[f, 1]
        send(acc.at[f, i, pl.ds(2, 2)], r2.at[f, 1, pl.ds(2, 2)], s2, (f, 1, 1), down)

    v[0], v[1] = inverse_lower([lower(h_ref[0, :NB]), lower(h_ref[1, NB:])])

    for d in range(3):
        arrive(m_x.at[d], sm, (1, d))
    m_b[...] = (m_a[r] + m_x[0] + (m_x[1] + m_x[2])).reshape(4, 32, 512)
    for d in range(3):
        send(m_b.at[(y + d + 1) % 4], m_y.at[d], sm, (2, d), yp[d])

    @pl.when(r == own_col)
    def _():
        for d in range(3):
            remote(col_x.at[d], col_x.at[d], sc.at[0, 0], sc.at[1, d], sibling).wait_recv()
        col_x[0] = col_ref[...] + col_x[0] + (col_x[1] + col_x[2])
        for index, target in enumerate(targets):
            b, h = index // 2, index % 2

            @pl.when(target != c)
            def _():
                remote(col_x.at[0, b, h], col_p, sp.at[0, index], sp.at[1, 0], {"row": r, "col": target}).start()

            @pl.when(target == c)
            def _():
                col_p[...] = col_x[0, b, h]

    for f in range(2):
        for side in range(2):
            for half in range(2):
                arrive(r2.at[f, side, pl.ds(2 * half, 2)], s2, (f, side, half))
        part[f] = acc[f, first[f]] + (r2[f, 0] + r2[f, 1])
        up, down = second_peers[f][0], second_peers[f][2]
        i = (second[f] + 2) % 4
        send(part.at[f, i, pl.ds(0, 32)], t1.at[f, 0], s3, (f, 0), up)
        send(part.at[f, i, pl.ds(32, 32)], t1.at[f, 1], s3, (f, 1), down)
        i = (second[f] + 1) % 4
        send(part.at[f, i, pl.ds(32, 32)], t2.at[f, 0, pl.ds(32, 32)], s4, (f, 0, 1), up)
        i = (second[f] + 3) % 4
        send(part.at[f, i, pl.ds(0, 32)], t2.at[f, 1, pl.ds(0, 32)], s4, (f, 1, 0), down)
    for d in range(3):
        arrive(m_y.at[d], sm, (2, d))
    m_c[...] = (m_b[y] + m_y[0] + (m_y[1] + m_y[2])).reshape(4, 8, 512)
    for d in range(3):
        send(m_c.at[(z + d + 1) % 4], m_z.at[d], sm, (3, d), zp[d])
    for f in range(2):
        up, down = second_peers[f][0], second_peers[f][2]
        i = (second[f] + 1) % 4
        arrive(t1.at[f, 0], s3, (f, 0))
        part[f, i, 0:32] = part[f, i, 0:32] + t1[f, 0]
        send(part.at[f, i, pl.ds(0, 32)], t2.at[f, 0, pl.ds(0, 32)], s4, (f, 0, 0), up)
        i = (second[f] + 3) % 4
        arrive(t1.at[f, 1], s3, (f, 1))
        part[f, i, 32:64] = part[f, i, 32:64] + t1[f, 1]
        send(part.at[f, i, pl.ds(32, 32)], t2.at[f, 1, pl.ds(32, 32)], s4, (f, 1, 1), down)
    for d in range(3):
        arrive(m_z.at[d], sm, (3, d))
    m_f[k, r, y, z] = m_c[z] + m_z[0] + (m_z[1] + m_z[2])
    for d in range(3):
        send(m_f.at[k, r, y, z], m_f.at[k, r, y, z], sm, (4, d), zp[d])

    @pl.when(source != c)
    def _():
        remote(col_p, col_p, sp.at[0, 0], sp.at[1, 0], sibling).wait_recv()

    def piece(f, i1, i2, half=None, h=None):
        h = k if h is None else h
        ref = o_ref.at[i2, i1, h, f] if f == 0 else o_ref.at[i1, i2, h, f]
        return ref if half is None else ref.at[pl.ds(half * 32, 32)]

    link = h_ref[0, NB:]
    for f in range(2):
        for side in range(2):
            for half in range(2):
                arrive(t2.at[f, side, pl.ds(32 * half, 32)], s4, (f, side, half))
        rows = part[f, second[f]] + (t2[f, 0] + t2[f, 1]) - col_p[f * 64:f * 64 + 64, :]
        last = dot(rows[:, NB:], v[1])
        piece(f, first[f], second[f])[...] = jnp.concatenate([dot(rows[:, :NB] - dot(last, link), v[0]), last], 1)
        mine = piece(f, first[f], second[f])
        send(mine, mine, g1, (f, 0), second_peers[f][0])
        send(mine, mine, g1, (f, 1), second_peers[f][2])
        for s, to in ((0, 0), (1, 2)):
            send(mine, mine, g2, (f, 0, s), first_peers[f][to])
        send(mine, mine, gs, (f, 0, 0), sibling)

    zs = [(z + 4 - d) % 4 for d in (1, 2, 3)]
    for d in range(3):
        arrive(m_f.at[k, r, y, zs[d]], sm, (4, d))
    for d in range(3):
        send(m_f.at[k, r, y], m_f.at[k, r, y], sm, (5, d), yp[d])

    for f in range(2):
        i1, i2 = first[f], second[f]
        back, ahead = piece(f, i1, (i2 + 3) % 4), piece(f, i1, (i2 + 1) % 4)
        arrive(back, g1, (f, 0))
        half = piece(f, i1, (i2 + 3) % 4, 0)
        send(half, half, g1, (f, 2), second_peers[f][0])
        arrive(ahead, g1, (f, 1))
        half = piece(f, i1, (i2 + 1) % 4, 1)
        send(half, half, g1, (f, 3), second_peers[f][2])
        for e, ref in ((3, back), (1, ahead)):
            for s, to in ((0, 0), (1, 2)):
                send(ref, ref, g2, (f, e, s), first_peers[f][to])
            send(ref, ref, gs, (f, e, 0), sibling)

    ys = [(y + 4 - d) % 4 for d in (1, 2, 3)]
    for d in range(3):
        arrive(m_f.at[k, r, ys[d]], sm, (5, d))
    for d in range(3):
        send(m_f.at[k, r], m_f.at[k, r], sm, (6, d), xp[d])

    def relay(f, e):
        i1, i2 = first[f], (second[f] + e) % 4
        for s, near, to in ((0, 3, 0), (1, 1, 2)):
            got = piece(f, (i1 + near) % 4, i2)
            arrive(got, g2, (f, e, s))
            half = piece(f, (i1 + near) % 4, i2, s)
            send(half, half, g2, (f, e, 2 + s), first_peers[f][to])
            send(got, got, gs, (f, e, 1 + s), sibling)

    for f in range(2):
        relay(f, 0)
    for f in range(2):
        i1, i2 = first[f], (second[f] + 2) % 4
        for s in range(2):
            arrive(piece(f, i1, i2, s), g1, (f, 2 + s))
        far = piece(f, i1, i2)
        for s, to in ((0, 0), (1, 2)):
            send(far, far, g2, (f, 2, s), first_peers[f][to])
        send(far, far, gs, (f, 2, 0), sibling)
    for e in (3, 1):
        for f in range(2):
            relay(f, e)
    rs = [(r + 4 - d) % 4 for d in (1, 2, 3)]
    for d in range(3):
        arrive(m_f.at[k, rs[d]], sm, (6, d))
    send(m_f.at[k], m_f.at[k], sm, (7, 0), sibling)
    for f in range(2):
        relay(f, 2)
    for e in (0, 3, 1, 2):
        for f in range(2):
            i1, i2 = first[f], (second[f] + e) % 4
            for s in range(2):
                arrive(piece(f, (i1 + 2) % 4, i2, s), g2, (f, e, 2 + s))
            far = piece(f, (i1 + 2) % 4, i2)
            send(far, far, gs, (f, e, 3), sibling)

    arrive(m_f.at[1 - k], sm, (7, 0))

    @pl.when(r < 2)
    def _():
        m = m_f[...].reshape(1024, 512)
        l0, l1, v0, v1 = lower(h_ref[0, :NB]), lower(h_ref[1, NB:]), v[0], v[1]
        g1q = tdot(v1, m[NB:512])
        g1q0, g1q1 = g1q[:, :NB], g1q[:, NB:]
        k1 = lower(m[512:768, NB:]) - lower(g1q1)
        e1 = tdot(v1, dot(lower_half(tdot(l1, k1)), v1))
        e1 = lower_half(e1 + e1.T)
        g01 = dot(m[512:768, :NB] - dot(e1 + e1.T, link) - g1q0, v0)

        @pl.when(r == 1)
        def _():
            top_ref[:, :NB] = g01
            top_ref[:, NB:] = e1

        @pl.when(r == 0)
        def _():
            g0q0 = tdot(v0, m[:NB, :NB] - tdot(link, g1q0)) + tdot(g01, link)
            k0 = lower(m[768:, :NB]) - lower(g0q0)
            e0 = tdot(v0, dot(lower_half(tdot(l0, k0)), v0))
            top_ref[:, :NB] = lower_half(e0 + e0.T)
            top_ref[:, NB:] = jnp.zeros((NB, NB), jnp.float32)

    @pl.when(r >= 2)
    def _():
        top_ref[...] = jnp.zeros((NB, 512), jnp.float32)

    for e in range(4):
        for f in range(2):
            i1, i2 = first[f], (second[f] + e) % 4
            for s, near in enumerate((0, 3, 1, 2)):
                arrive(piece(f, (i1 + near) % 4, i2, None, 1 - k), gs, (f, e, s))
    for copy in sent:
        copy.wait_send()

    @pl.when(r != own_col)
    def _():
        remote(col_ref, col_ref, sc.at[0, 0], sc.at[1, 0], sibling).wait_send()

    @pl.when(r == own_col)
    def _():
        for index, target in enumerate(targets):
            @pl.when(target != c)
            def _():
                remote(col_p, col_p, sp.at[0, index], sp.at[1, 0], sibling).wait_send()


def reduce_and_gather(w, col_part, m_part, heads):
    f32 = jnp.float32
    vmem, dma = pltpu.VMEM, pltpu.SemaphoreType.DMA
    here = pl.BlockSpec(memory_space=pltpu.VMEM)
    o, top = pl.pallas_call(
        reduce_kernel,
        out_shape=(jax.ShapeDtypeStruct((4, 4, 2, 2, 64, 512), f32), jax.ShapeDtypeStruct((NB, 512), f32)),
        in_specs=[here] * 4,
        out_specs=(here, here),
        scratch_shapes=[
            vmem((2, 4, 4, 64, 512), f32), vmem((2, 4, 4, 64, 512), f32), vmem((2, 2, 2, 64, 512), f32), vmem((2, 2, 4, 64, 512), f32),
            vmem((2, 4, 64, 512), f32), vmem((2, 2, 32, 512), f32), vmem((2, 2, 64, 512), f32), vmem((2, NB, NB), f32),
            vmem((3, 2, 2, 128, 512), f32), vmem((128, 512), f32), vmem((4, 128, 512), f32), vmem((4, 128, 512), f32),
            vmem((3, 128, 512), f32), vmem((4, 32, 512), f32), vmem((3, 32, 512), f32), vmem((4, 8, 512), f32), vmem((3, 8, 512), f32),
            vmem((2, 4, 4, 4, 8, 512), f32),
            dma((2, 2, 4)), dma((2, 2, 2)), dma((2, 2, 2, 2)), dma((2, 2, 2)), dma((2, 2, 2, 2)), dma((2, 3)), dma((2, 4)),
            dma((2, 8, 3)), dma((2, 2, 4)), dma((2, 2, 4, 4)), dma((2, 2, 4, 4)),
        ],
        compiler_params=pltpu.CompilerParams(collective_id=2, has_side_effects=True, vmem_limit_bytes=60 << 20),
    )(w.reshape(4, 4, 2, 2, 64, 512), col_part.reshape(2, 2, 128, 512), m_part.reshape(2, 4, 128, 512), heads)
    return o.reshape(ROWS, 512), top


def local(factor, adjoint):
    row_id = lax.axis_index("row")
    p, q = broadcast(factor)
    w, col_part, m_part = products(adjoint, p, q)
    out, top = reduce_and_gather(w, col_part, m_part, p[:, ROWS:])
    return jnp.concatenate([jnp.where(row_id < 2, top, out[:NB]), out[NB:]], 0)


def solution(mesh):
    placed = (P("row", "col"), P("row", "col"))
    return jax.shard_map(local, mesh=mesh, in_specs=placed, out_specs=P("row", None), check_vma=False)
```

time: 1200 us -> 217 us (0.18); the launches traced: 1180 us -> 217 us
  between operations: 515 us -> 0.05 us
  waiting for transfers between devices: 359 us -> 0 us
  matrix products: 214 us -> 0 us
  Pallas kernels: 0 us -> 196 us
  other arithmetic: 49.1 us -> 5.66 us
  local copies, waits for them, and re-layouts: 47.6 us -> 15.6 us
    psum x5 -> x0, waiting for transfers between devices: 309 us -> none  [the longest x1 124 us: from_root(): return lax.psum(block, axis)]
    dot_general x525 -> x0, matrix products: 214 us -> none  [the longest x516 144 us: matmul(): jnp.dot(left_side, right_side, precision=HIGHEST_PRECISION, preferred_ele...]
    pallas_call x0 -> x3, Pallas kernels: none -> 196 us  [the longest x1 121 us: reduce_and_gather(): pl.pallas_call(reduce_kernel, out_shape=(jax.ShapeDtypeStruct((4, 4, 2, 2...]
    all_gather x4 -> x0, waiting for transfers between devices: 49.7 us -> none  [the longest x1 26.4 us: local(): lax.all_gather(y_second[:NB], 'row', axis=0, tiled=True)]
    slice x48 -> x2, local copies, waits for them, and re-layouts: 38.9 us -> 6.48 us  [the longest x1 4.15 us: local(): return jnp.concatenate([jnp.where(row_id < 2, top, out[:NB]), out[NB:]], 0)]
    select_n x7 -> x1, other arithmetic: 24.9 us -> 1.29 us  [local(): return jnp.concatenate([jnp.where(row_id < 2, top, out[:NB]), out[NB:]], 0)]
    concatenate x207 -> x1, other arithmetic: 22 us -> 4.38 us  [local(): return jnp.concatenate([jnp.where(row_id < 2, top, out[:NB]), out[NB:]], 0)]
  transfers between devices with their start and end apart: 9 -> 0, of which waited for: 6 -> 0; matrix products, arithmetic and copies ran while one was open for 19% -> 0% of each run, Pallas kernels for 0% -> 0%
where the time goes in v1:
time: 217 us
  Pallas kernels  196 us (90%)
  local copies, waits for them, and re-layouts  15.6 us (7%)
  other arithmetic  5.66 us (3%)
    pallas_call x1, Pallas kernels, reduce_and_gather(): pl.pallas_call(reduce_kernel, out_shape=(jax.ShapeDtypeStruct((4, 4, 2, 2...  121 us
    pallas_call x1, Pallas kernels, broadcast(): pl.pallas_call(broadcast_kernel, out_shape=(jax.ShapeDtypeStruct((2, ROWS...  53.1 us
    pallas_call x1, Pallas kernels, products(): pl.pallas_call(product_kernel, out_shape=(jax.ShapeDtypeStruct((ROWS, 512...  21.2 us
    unnamed x8, local copies, waits for them, and re-layouts  9.09 us
    concatenate x1, other arithmetic, local(): return jnp.concatenate([jnp.where(row_id < 2, top, out[:NB]), out[NB:]], 0)  4.38 us

profile of v1, /device:TPU:0, one launch (start us, length us, event | category | flops | bytes accessed | tf_op | source)
XLA Modules:
  0.0 217.0 jit_solution(8922278198123123181)
XLA Ops:
  0.0 0.0 copy-start.1
  0.0 3.4 %copy-done.1 = f32[4096,512]{1,0:T(8,128)S(1)} copy-done((f32[4096,512]{1,0:T(8,128)S(1)}, f32[4096,512]{1,0:T(8,128)}, u32[]{:S(2)}) %copy-start.1) | copy-done | bytes 8388632
  3.4 53.1 %shard_map.28 = (f32[2,4608,256]{2,1,0:T(8,128)}, f32[2,512,256]{2,1,0:T(8,128)S(1)}) custom-call(f32[4096,512]{1,0:T(8,128)S(1)} %copy-done.1), custom_call_target="tpu_custom_call" | custom-call | tf_op jit(solution)/shard_map/pallas_call | solution.py:220
  56.5 21.2 %shard_map.29 = (f32[4096,512]{1,0:T(8,128)S(1)}, f32[2,256,512]{2,1,0:T(8,128)S(1)}, f32[1024,512]{1,0:T(8,128)S(1)}) custom-call(f32[4096,512]{1,0:T(8,128)} %a_ref.1, f32[2,4608,256]{2,1,0:T(8,128)} %get-tuple-element.12.p_ref, f32[2,512,256]{2,1,0:T(8,128)S(1)} %get-tuple-element.13.q_ref), custom_call_target="tpu_custom_call" | custom-call | tf_op jit(solution)/shard_map/pallas_call | solution.py:300
  77.7 0.0 copy-start
  77.7 3.4 %copy-done = f32[4096,512]{1,0:T(8,128)} copy-done((f32[4096,512]{1,0:T(8,128)}, f32[4096,512]{1,0:T(8,128)S(1)}, u32[]{:S(2)}) %copy-start) | copy-done | bytes 8388632
  81.1 0.0 copy-start.2
  81.1 1.3 copy-done.2
  82.4 0.0 copy-start.3
  82.4 1.0 copy-done.3
  83.4 2.3 %slice.9.h_ref = f32[2,512,256]{2,1,0:T(8,128)} slice(f32[2,4608,256]{2,1,0:T(8,128)} %get-tuple-element.12.p_ref), slice={[0:2], [4096:4608], [0:256]} | slice | bytes 2097152 | tf_op jit(solution)/shard_map/slice | solution.py:616
  85.8 121.4 %shard_map.30 = (f32[4,4,2,2,64,512]{5,4,3,2,1,0:T(8,128)}, f32[256,512]{1,0:T(8,128)}) custom-call(f32[4,4,2,2,64,512]{5,4,3,2,1,0:T(8,128)} %bitcast.4, f32[2,2,128,512]{3,2,1,0:T(8,128)} %bitcast.6, f32[2,4,128,512]{3,2,1,0:T(8,128)} %bitcast.5, f32[2,512,256]{2,1,0:T(8,128)} %slice.9.h_ref), custom_call_target="tpu_custom_call" | custom-call | tf_op jit(solution)/shard_map/pallas_call | solution.py:593
  207.2 1.3 slice_select_fusion
  208.5 4.1 %slice.13 = f32[3840,512]{1,0:T(8,128)S(1)} slice(f32[4096,512]{1,0:T(8,128)} %bitcast.8), slice={[256:4096], [0:512]} | slice | bytes 15728640 | tf_op jit(solution)/shard_map/slice | solution.py:617
  212.6 4.4 %pad_maximum_fusion = f32[4096,512]{1,0:T(8,128)} fusion(f32[3840,512]{1,0:T(8,128)S(1)} %slice.13, f32[256,512]{1,0:T(8,128)S(1)} %slice_select_fusion), kind=kLoop, calls=%fused_computation | loop fusion | flops 2097152 | bytes 16777216 | tf_op jit(solution)/shard_map/concatenate | solution.py:617
Async XLA Ops:
  0.0 3.4 %copy-start.1 = (f32[4096,512]{1,0:T(8,128)S(1)}, f32[4096,512]{1,0:T(8,128)}, u32[]{:S(2)}) copy-start(f32[4096,512]{1,0:T(8,128)} %f_ref.1) | copy-start | bytes 25165828
  77.7 3.4 %copy-start = (f32[4096,512]{1,0:T(8,128)}, f32[4096,512]{1,0:T(8,128)S(1)}, u32[]{:S(2)}) copy-start(f32[4096,512]{1,0:T(8,128)S(1)} %get-tuple-element.14) | copy-start | bytes 25165828
  81.1 1.3 copy-start.2
  82.4 1.0 copy-start.3

commit v2 on v1

--- a/solution.py
+++ b/solution.py
@@ -32,25 +32,9 @@
     return jnp.where(i > j, x, jnp.where(i == j, 0.5 * x, 0.0))
 
 
-def inverse_lower(mats):
-    n = mats[0].shape[0]
-    i, j = grid_ids(n)
-    found = []
-    for m in mats:
-        d = jnp.where(i == j, m, 0.0)
-        found.append(jnp.where(i == j, 1.0 / jnp.where(i == j, m, 1.0), 0.0))
-    k = 1
-    while k < n:
-        corner = (i // (2 * k) == j // (2 * k)) & (i // k > j // k)
-        inner = [dot(jnp.where(corner, m, 0.0), x) for m, x in zip(mats, found)]
-        found = [x - dot(x, y) for x, y in zip(found, inner)]
-        k *= 2
-    return found
-
-
 MESH = pl.DeviceIdType.MESH
 ROWS, HEAD, CHUNK = 4096, 512, 32
-STEPS, LAG = 36, 5
+STEPS, LAG, AHEAD = 36, 5, 16
 DEPTH = ((0, 3, 4, 3, 3, 4, 5, 4, 2, 3, 4, 3, 1, 2, 3, 2), (0, 3, 2, 1, 3, 4, 3, 2, 4, 5, 4, 3, 3, 4, 3, 2),
          (0, 3, 4, 3, 1, 2, 3, 2, 2, 3, 4, 3, 3, 4, 5, 4), (0, 1, 2, 3, 3, 2, 3, 4, 4, 3, 4, 5, 3, 2, 3, 4))
 TREE_OF_LINK = ((2, 3, 3, 1, 2, 2, 3, 1, 2, 2, 2, 2, 9, 0, 0, 0), (3, 3, 3, 9, 2, 2, 3, 1, 0, 0, 3, 1, 0, 3, 3, 1),
@@ -93,27 +77,32 @@
     sibling = at(r, y, z, 1 - k)
     nexts = [at(r, (y + dy) % 4, (z + dz) % 4, k) for dy, dz in LINKS]
     xs = [at((r + d) % 4, y, z, k) for d in (1, 3, 2)]
+    load = pltpu.make_async_copy(f_ref.at[:, pl.ds(0, NB)], p_ref.at[k, pl.ds(0, ROWS), :], own.at[0])
+
+    @pl.when(chip == 0)
+    def _():
+        load.start()
+
     meet(nexts + [sibling] + xs)
     depth = [pick(chip, row) for row in DEPTH]
     tree = [pick(chip, row) for row in TREE_OF_LINK]
     is_root = chip == 0
 
     def first_row(s, t):
-        u = jnp.where(s < 8, s, s - 4)
+        u = jnp.where(s < AHEAD, s, s - 4)
         body = ((u % 8) * 2 + t // 2) * NB + (u // 8) * 64 + (t % 2) * CHUNK
-        head = ROWS + ((s - 8) * 4 + t) * CHUNK
-        return pl.multiple_of(jnp.where((s >= 8) & (s < 12), head, body), CHUNK)
+        head = ROWS + ((s - AHEAD) * 4 + t) * CHUNK
+        return pl.multiple_of(jnp.where((s >= AHEAD) & (s < AHEAD + 4), head, body), CHUNK)
 
     def pass_on(s, t, src, dst):
-        remote(src, dst, sib_send.at[s, t], sib_recv.at[s, t], sibling).start()
         for d in range(4):
             @pl.when(tree[d] == t)
             def _():
                 remote(src, dst, send.at[d, s], recv.at[s, t], nexts[d]).start()
+        remote(src, dst, sib_send.at[s, t], sib_recv.at[s, t], sibling).start()
 
     @pl.when(is_root)
     def _():
-        pltpu.make_async_copy(f_ref.at[:, pl.ds(0, NB)], p_ref.at[k, pl.ds(0, ROWS), :], own.at[0]).start()
         for head in range(2):
             rows = p_ref.at[k, pl.ds(ROWS + head * NB, NB), :]
             block = f_ref.at[pl.ds(0, NB), pl.ds(0, NB)]
@@ -129,8 +118,8 @@
                 rows = p_ref.at[k, pl.ds(first_row(s, t), CHUNK), :]
                 pass_on(s, t, rows, rows)
 
-        pltpu.make_async_copy(f_ref.at[:, pl.ds(0, NB)], p_ref.at[k, pl.ds(0, ROWS), :], own.at[0]).wait()
-        lax.fori_loop(0, 8, from_own, None)
+        load.wait()
+        lax.fori_loop(0, AHEAD, from_own, None)
         for head in range(2):
             rows = p_ref.at[k, pl.ds(ROWS + head * NB, NB), :]
 
@@ -144,7 +133,7 @@
             def _():
                 remote(rows, rows, h_send.at[0], h_recv.at[head], xs[0]).wait_recv()
 
-        lax.fori_loop(8, STEPS, from_own, None)
+        lax.fori_loop(AHEAD, STEPS, from_own, None)
 
     def forward(n, _):
         for t in range(4):
@@ -157,7 +146,7 @@
                 pass_on(s, t, rows, rows)
 
     m = c // 4
-    stops = [8 + LAG * 4, 20 + LAG * 4, 28 + LAG * 4, 36 + LAG * 4]
+    stops = [8 * j + 8 + (4 if 8 * j + 8 > AHEAD else 0) + LAG * 4 for j in range(4)]
     for j in range(4):
         @pl.when(jnp.logical_not(is_root))
         def _():
@@ -167,7 +156,7 @@
         def _():
             for b in range(2):
                 row = pl.multiple_of((m + 8 * b) * NB + j * 64, 64)
-                s = (j * 8 + 4 * b + m // 2) + (4 if j else 0)
+                s = (j * 8 + 4 * b + m // 2) + (4 if 8 * j >= AHEAD else 0)
                 for half in range(2):
                     t = (m % 2) * 2 + half
                     got = p_ref.at[1 - k, pl.ds(row + half * CHUNK, CHUNK), :]
@@ -184,9 +173,9 @@
             mine = p_ref.at[k, pl.ds(row, CHUNK), :]
             other = p_ref.at[1 - k, pl.ds(row, CHUNK), :]
             remote(mine, mine, sib_send.at[s, t], sib_recv.at[s, t], sibling).wait_send()
-            u = jnp.where(s < 8, s, s - 4)
+            u = jnp.where(s < AHEAD, s, s - 4)
             block = (u % 8) * 2 + t // 2
-            early = (r == c % 4) & ((s < 8) | (s >= 12)) & (block % 8 == m)
+            early = (r == c % 4) & ((s < AHEAD) | (s >= AHEAD + 4)) & (block % 8 == m)
 
             @pl.when(jnp.logical_not(early))
             def _():
@@ -216,15 +205,14 @@
 
 def broadcast(factor):
     dma = pltpu.SemaphoreType.DMA
-    anywhere = pl.BlockSpec(memory_space=pl.ANY)
     return pl.pallas_call(
         broadcast_kernel,
         out_shape=(jax.ShapeDtypeStruct((2, ROWS + HEAD, NB), jnp.float32), jax.ShapeDtypeStruct((2, 512, NB), jnp.float32)),
-        in_specs=[anywhere],
+        in_specs=[pl.BlockSpec(memory_space=pltpu.HBM)],
         out_specs=(pl.BlockSpec(memory_space=pltpu.VMEM),) * 2,
         scratch_shapes=[dma((4, STEPS)), dma((STEPS, 4)), dma((STEPS, 4)), dma((STEPS, 4)), dma((4, 2, 3)), dma((4, 2)),
                         dma((3,)), dma((2,)), dma((10,))],
-        compiler_params=pltpu.CompilerParams(collective_id=1, has_side_effects=True, vmem_limit_bytes=40 << 20),
+        compiler_params=pltpu.CompilerParams(collective_id=1, has_side_effects=True, vmem_limit_bytes=60 << 20),
     )(factor)
 
 
@@ -239,80 +227,21 @@
     return one(a[0], b[0]) + (one(a[0], b[1]) + one(a[1], b[0]))
 
 
-def product_kernel(a_ref, p_ref, q_ref, w_ref, col_ref, m_ref, row_acc, qh, ql):
-    step = pl.program_id(0)
-    r, c = lax.axis_index("row"), lax.axis_index("col")
-    block = 4 * step + r
+def inverse_first(mats):
     i, j = grid_ids(NB)
-
-    @pl.when(step == 0)
-    def _():
-        col_ref[...] = jnp.zeros_like(col_ref)
-        m_ref[...] = jnp.zeros_like(m_ref)
-        for b in range(2):
-            for k in range(2):
-                qh[b, :, k * NB:(k + 1) * NB], ql[b, :, k * NB:(k + 1) * NB] = split(q_ref[k, b * NB:(b + 1) * NB, :])
-        for head, (hr, hc, lo, side) in enumerate([(0, 0, 768, 0), (1, 0, 512, 0), (1, 1, 512, NB)]):
-            @pl.when((r == hr) & (c == hc))
-            def _():
-                m_ref[lo:lo + NB, side:side + NB] = a_ref[:, :NB]
-
-    row_acc[...] = jnp.zeros_like(row_acc)
-    panel = split(jnp.concatenate([p_ref[0], p_ref[1]], 1))
-    for b in range(2):
-        column = 32 * b + c
-        owner = (column < 2)
-
-        @pl.when((block >= column) & (block >= 2))
-        def _():
-            tile = a_ref[:, b * NB:(b + 1) * NB]
-            tile = jnp.where((block > column) | (i >= j), tile, 0.0)
-            tile = split(tile)
-            col_ref[b] += dot3(tile, panel, ((0,), (0,)))
-
-            @pl.when(jnp.logical_not(owner))
-            def _():
-                row_acc[...] += dot3(tile, (qh[b], ql[b]), ((1,), (0,)))
-
-    for side in range(2):
-        part = slice(side * NB, (side + 1) * NB)
-        own = jnp.where(c == side, a_ref[:, :NB], 0.0)
-        w_ref[:, part] = own - row_acc[:, part]
-
-    @pl.when(step == pl.num_programs(0) - 1)
-    def _():
-        for side in range(2):
-            @pl.when(c == side)
-            def _():
-                m_ref[side * NB:(side + 1) * NB, :] = col_ref[0]
-
-        @pl.when(c < 2)
-        def _():
-            col_ref[0] = jnp.zeros((NB, 512), jnp.float32)
-
-        s = jnp.zeros((512, 512), jnp.float32)
-        for b in range(2):
-            s += dot3(split(col_ref[b]), (qh[b], ql[b]), ((0,), (0,)))
-        m_ref[:512] += -s - s.T
-
-
-def products(adjoint, p, q):
-    return pl.pallas_call(
-        product_kernel,
-        out_shape=(jax.ShapeDtypeStruct((ROWS, 512), jnp.float32), jax.ShapeDtypeStruct((2, NB, 512), jnp.float32),
-                   jax.ShapeDtypeStruct((1024, 512), jnp.float32)),
-        grid=(16,),
-        in_specs=[pl.BlockSpec((NB, 512), lambda a: (a, 0)), pl.BlockSpec((2, NB, NB), lambda a: (0, a, 0)),
-                  pl.BlockSpec((2, 512, NB), lambda a: (0, 0, 0))],
-        out_specs=(pl.BlockSpec((NB, 512), lambda a: (a, 0)), pl.BlockSpec((2, NB, 512), lambda a: (0, 0, 0)),
-                   pl.BlockSpec((1024, 512), lambda a: (0, 0))),
-        scratch_shapes=[pltpu.VMEM((NB, 512), jnp.float32), pltpu.VMEM((2, NB, 512), jnp.bfloat16), pltpu.VMEM((2, NB, 512), jnp.bfloat16)],
-        compiler_params=pltpu.CompilerParams(vmem_limit_bytes=40 << 20),
-    )(adjoint, p, q)
-
-
-def reduce_kernel(w_ref, col_ref, m_ref, h_ref, o_ref, top_ref, acc, sib, r1, r2, part, t1, t2, v, col_x, col_p, m_a, m_s, m_x, m_b,
-                  m_y, m_c, m_z, m_f, s0, s1, s2, s3, s4, sc, sp, sm, g1, g2, gs):
+    d = [jnp.where(i == j, 1.0 / jnp.where(i == j, m, 1.0), 0.0) for m in mats]
+    return inverse_level(mats, d, 1)
+
+
+def inverse_level(mats, found, size):
+    i, j = grid_ids(NB)
+    corner = (i // (2 * size) == j // (2 * size)) & (i // size > j // size)
+    inner = [dot(jnp.where(corner, m, 0.0), x) for m, x in zip(mats, found)]
+    return [x - dot(x, y) for x, y in zip(found, inner)]
+
+
+def main_kernel(a_hbm, p_hbm, q_ref, o_ref, top_ref, a_ref, p_ref, h_ref, qh, ql, row_acc, w_ref, col_ref, m_ref, acc, sib, r1, r2, part, t1, t2, v, col_x, col_p, m_a, m_s, m_x, m_b,
+                  m_y, m_c, m_z, m_f, sl, s0, s1, s2, s3, s4, sc, sp, sm, g1, g2, gs):
     r, c, y, z, k = place()
     sibling = at(r, y, z, 1 - k)
     xp = [at((r + d) % 4, y, z, k) for d in (1, 2, 3)]
@@ -333,6 +262,63 @@
     @pl.when(source != c)
     def _():
         pl.semaphore_signal(barrier, inc=1, device_id={"row": r, "col": source}, device_id_type=MESH)
+
+    def load_a(a):
+        rows = pl.ds(pl.multiple_of(a * NB, NB), NB)
+        return pltpu.make_async_copy(a_hbm.at[rows], a_ref.at[a], sl.at[a])
+
+    def load_p(a):
+        rows = pl.ds(pl.multiple_of(a * NB, NB), NB)
+        return pltpu.make_async_copy(p_hbm.at[:, rows], p_ref.at[a % 2], sl.at[16 + a % 2])
+
+    load_h = pltpu.make_async_copy(p_hbm.at[:, pl.ds(ROWS, HEAD)], h_ref, sl.at[18])
+    load_p(0).start()
+    for a in range(16):
+        load_a(a).start()
+    load_h.start()
+    i_ids, j_ids = grid_ids(NB)
+    col_ref[...] = jnp.zeros_like(col_ref)
+    m_ref[...] = jnp.zeros_like(m_ref)
+    for b in range(2):
+        for side in range(2):
+            qh[b, :, side * NB:(side + 1) * NB], ql[b, :, side * NB:(side + 1) * NB] = split(q_ref[side, b * NB:(b + 1) * NB, :])
+
+    def tile_of(a, b):
+        column = 32 * b + c
+        tile = a_ref[a, :, b * NB:(b + 1) * NB]
+        return split(jnp.where((4 * a + r > column) | (i_ids >= j_ids), tile, 0.0))
+
+    def column_step(a, _):
+        @pl.when(a < 15)
+        def _():
+            load_p(a + 1).start()
+        load_a(a).wait()
+        load_p(a).wait()
+        panel = split(jnp.concatenate([p_ref[a % 2, 0], p_ref[a % 2, 1]], 1))
+        for b in range(2):
+            @pl.when((4 * a + r >= 32 * b + c) & (4 * a + r >= 2))
+            def _():
+                col_ref[b] += dot3(tile_of(a, b), panel, ((0,), (0,))).reshape(2, 128, 512)
+
+    lax.fori_loop(0, 16, column_step, None)
+    for hr, hc, lo, side in ((0, 0, 2, 0), (1, 0, 0, 0), (1, 1, 0, NB)):
+        @pl.when((r == hr) & (c == hc))
+        def _():
+            m_ref[1, lo:lo + 2, :, side:side + NB] = a_ref[0, :, :NB].reshape(2, 128, NB)
+    for side in range(2):
+        @pl.when(c == side)
+        def _():
+            m_ref[0, 2 * side:2 * side + 2] = col_ref[0]
+
+    @pl.when(c < 2)
+    def _():
+        col_ref[0] = jnp.zeros((2, 128, 512), jnp.float32)
+
+    gram = jnp.zeros((512, 512), jnp.float32)
+    for b in range(2):
+        gram += dot3(split(col_ref[b].reshape(NB, 512)), (qh[b], ql[b]), ((0,), (0,)))
+    m_ref[0] += (-gram - gram.T).reshape(4, 128, 512)
+    load_h.wait()
     pl.semaphore_wait(barrier, 10 + others)
 
     sent = []
@@ -345,6 +331,13 @@
     def arrive(dst, sems, index):
         remote(dst, dst, sems.at[(0, *index)], sems.at[(1, *index)], sibling).wait_recv()
 
+    def invert(stage):
+        low = [lower(h_ref[0, :NB]), lower(h_ref[1, NB:])]
+        found = inverse_first(low) if stage == 0 else [v[0], v[1]]
+        for size in ((2, 4), (8, 16, 32), (64, 128))[stage]:
+            found = inverse_level(low, found, size)
+        v[0], v[1] = found
+
     first = [z, y]
     second = [y, z]
     first_peers, second_peers = [zp, yp], [yp, zp]
@@ -353,21 +346,52 @@
         return w_ref.at[:, i, h, 0] if f == 0 else w_ref.at[i, :, h, 1]
 
     send(m_ref.at[1 - k], m_s, sm, (0, 0), sibling)
-    for j in (2, 1, 3, 0):
-        for f in range(2):
-            i = (first[f] + j) % 4
-            send(w_shard(f, 1 - k, i), sib.at[f, i], s0, (f, j), sibling)
-
-    @pl.when(r != own_col)
-    def _():
-        slot = (own_col - r + 4) % 4 - 1
-        remote(col_ref, col_x.at[slot], sc.at[0, 0], sc.at[1, slot], {"row": own_col, "col": c}).start()
-
     arrive(m_s, sm, (0, 0))
     m_a[...] = m_ref[k] + m_s[...]
     for d in range(3):
         send(m_a.at[(r + d + 1) % 4], m_x.at[d], sm, (1, d), xp[d])
 
+    gap = (own_col - r + 4) % 4
+
+    def col_copy(b, slot, device, which):
+        return remote(col_ref.at[b], col_x.at[slot, b], sc.at[0, which], sc.at[1, 2 * slot + b], device)
+
+    @pl.when(gap == 2)
+    def _():
+        col_copy(0, 2, xp[2], 0).start()
+        col_copy(1, 2, xp[0], 1).start()
+
+    @pl.when(gap == 3)
+    def _():
+        col_copy(1, 0, xp[2], 0).start()
+
+    @pl.when(gap == 1)
+    def _():
+        col_copy(0, 1, xp[0], 0).start()
+
+    def row_step(row_y, row_z):
+        a = 4 * row_y + row_z
+        row_acc[...] = jnp.zeros_like(row_acc)
+        for b in range(2):
+            column = 32 * b + c
+
+            @pl.when((4 * a + r >= column) & (column >= 2))
+            def _():
+                row_acc[...] += dot3(tile_of(a, b), (qh[b], ql[b]), ((1,), (0,)))
+        for side in range(2):
+            part_of = slice(side * NB, (side + 1) * NB)
+            own = jnp.where(c == side, a_ref[a, :, :NB], 0.0)
+            w_ref[row_y, row_z, :, :, :, part_of] = (own - row_acc[:, part_of]).reshape(2, 2, 64, NB)
+
+    for j in (2, 1, 3, 0):
+        def one(row_y, _):
+            row_step(row_y, (z + j) % 4)
+        lax.fori_loop(0, 4, one, None)
+        i = (z + j) % 4
+        send(w_shard(0, 1 - k, i), sib.at[0, i], s0, (0, j), sibling)
+    for j in (2, 1, 3, 0):
+        i = (y + j) % 4
+        send(w_shard(1, 1 - k, i), sib.at[1, i], s0, (1, j), sibling)
     for j in (2, 1, 3, 0):
         for f in range(2):
             i = (first[f] + j) % 4
@@ -381,6 +405,19 @@
                 send(acc.at[f, i, pl.ds(2, 2)], r2.at[f, 0, pl.ds(2, 2)], s2, (f, 0, 1), up)
             if j == 3:
                 send(acc.at[f, i, pl.ds(0, 2)], r2.at[f, 1, pl.ds(0, 2)], s2, (f, 1, 0), down)
+    @pl.when(gap == 3)
+    def _():
+        col_copy(0, 2, xp[2], 1).wait_recv()
+        col_ref[0] = col_ref[0] + col_x[2, 0]
+        col_copy(0, 0, xp[2], 1).start()
+
+    @pl.when(gap == 1)
+    def _():
+        col_copy(1, 2, xp[0], 1).wait_recv()
+        col_ref[1] = col_ref[1] + col_x[2, 1]
+        col_copy(1, 1, xp[0], 1).start()
+
+    invert(0)
     for f in range(2):
         up, down = first_peers[f][0], first_peers[f][2]
         i = (first[f] + 1) % 4
@@ -392,30 +429,14 @@
         acc[f, i, 2:4] = acc[f, i, 2:4] + r1[f, 1]
         send(acc.at[f, i, pl.ds(2, 2)], r2.at[f, 1, pl.ds(2, 2)], s2, (f, 1, 1), down)
 
-    v[0], v[1] = inverse_lower([lower(h_ref[0, :NB]), lower(h_ref[1, NB:])])
-
+    invert(1)
     for d in range(3):
         arrive(m_x.at[d], sm, (1, d))
     m_b[...] = (m_a[r] + m_x[0] + (m_x[1] + m_x[2])).reshape(4, 32, 512)
     for d in range(3):
         send(m_b.at[(y + d + 1) % 4], m_y.at[d], sm, (2, d), yp[d])
 
-    @pl.when(r == own_col)
-    def _():
-        for d in range(3):
-            remote(col_x.at[d], col_x.at[d], sc.at[0, 0], sc.at[1, d], sibling).wait_recv()
-        col_x[0] = col_ref[...] + col_x[0] + (col_x[1] + col_x[2])
-        for index, target in enumerate(targets):
-            b, h = index // 2, index % 2
-
-            @pl.when(target != c)
-            def _():
-                remote(col_x.at[0, b, h], col_p, sp.at[0, index], sp.at[1, 0], {"row": r, "col": target}).start()
-
-            @pl.when(target == c)
-            def _():
-                col_p[...] = col_x[0, b, h]
-
+    invert(2)
     for f in range(2):
         for side in range(2):
             for half in range(2):
@@ -444,6 +465,23 @@
         arrive(t1.at[f, 1], s3, (f, 1))
         part[f, i, 32:64] = part[f, i, 32:64] + t1[f, 1]
         send(part.at[f, i, pl.ds(32, 32)], t2.at[f, 1, pl.ds(32, 32)], s4, (f, 1, 1), down)
+    @pl.when(r == own_col)
+    def _():
+        for slot in range(2):
+            for b in range(2):
+                col_copy(b, slot, sibling, 0).wait_recv()
+        col_x[0] = col_ref[...] + (col_x[0] + col_x[1])
+        for index, target in enumerate(targets):
+            b, h = index // 2, index % 2
+
+            @pl.when(target != c)
+            def _():
+                remote(col_x.at[0, b, h], col_p, sp.at[0, index], sp.at[1, 0], {"row": r, "col": target}).start()
+
+            @pl.when(target == c)
+            def _():
+                col_p[...] = col_x[0, b, h]
+
     for d in range(3):
         arrive(m_z.at[d], sm, (3, d))
     m_f[k, r, y, z] = m_c[z] + m_z[0] + (m_z[1] + m_z[2])
@@ -498,7 +536,9 @@
     for d in range(3):
         arrive(m_f.at[k, r, ys[d]], sm, (5, d))
     for d in range(3):
-        send(m_f.at[k, r], m_f.at[k, r], sm, (6, d), xp[d])
+        @pl.when((r + d + 1) % 4 < 2)
+        def _():
+            remote(m_f.at[k, r], m_f.at[k, r], sm.at[0, 6, d], sm.at[1, 6, d], xp[d]).start()
 
     def relay(f, e):
         i1, i2 = first[f], (second[f] + e) % 4
@@ -523,23 +563,18 @@
         for f in range(2):
             relay(f, e)
     rs = [(r + 4 - d) % 4 for d in (1, 2, 3)]
-    for d in range(3):
-        arrive(m_f.at[k, rs[d]], sm, (6, d))
-    send(m_f.at[k], m_f.at[k], sm, (7, 0), sibling)
+
+    @pl.when(r < 2)
+    def _():
+        for d in range(3):
+            arrive(m_f.at[k, rs[d]], sm, (6, d))
+        remote(m_f.at[k], m_f.at[k], sm.at[0, 7, 0], sm.at[1, 7, 0], sibling).start()
+
     for f in range(2):
         relay(f, 2)
-    for e in (0, 3, 1, 2):
-        for f in range(2):
-            i1, i2 = first[f], (second[f] + e) % 4
-            for s in range(2):
-                arrive(piece(f, (i1 + 2) % 4, i2, s), g2, (f, e, 2 + s))
-            far = piece(f, (i1 + 2) % 4, i2)
-            send(far, far, gs, (f, e, 3), sibling)
-
-    arrive(m_f.at[1 - k], sm, (7, 0))
-
     @pl.when(r < 2)
     def _():
+        arrive(m_f.at[1 - k], sm, (7, 0))
         m = m_f[...].reshape(1024, 512)
         l0, l1, v0, v1 = lower(h_ref[0, :NB]), lower(h_ref[1, NB:]), v[0], v[1]
         g1q = tdot(v1, m[NB:512])
@@ -566,6 +601,14 @@
     def _():
         top_ref[...] = jnp.zeros((NB, 512), jnp.float32)
 
+    for e in (0, 3, 1, 2):
+        for f in range(2):
+            i1, i2 = first[f], (second[f] + e) % 4
+            for s in range(2):
+                arrive(piece(f, (i1 + 2) % 4, i2, s), g2, (f, e, 2 + s))
+            far = piece(f, (i1 + 2) % 4, i2)
+            send(far, far, gs, (f, e, 3), sibling)
+
     for e in range(4):
         for f in range(2):
             i1, i2 = first[f], (second[f] + e) % 4
@@ -573,10 +616,19 @@
                 arrive(piece(f, (i1 + near) % 4, i2, None, 1 - k), gs, (f, e, s))
     for copy in sent:
         copy.wait_send()
+    for d in range(3):
+        @pl.when((r + d + 1) % 4 < 2)
+        def _():
+            remote(m_f.at[k, r], m_f.at[k, r], sm.at[0, 6, d], sm.at[1, 6, d], xp[d]).wait_send()
+
+    @pl.when(r < 2)
+    def _():
+        remote(m_f.at[k], m_f.at[k], sm.at[0, 7, 0], sm.at[1, 7, 0], sibling).wait_send()
 
     @pl.when(r != own_col)
     def _():
-        remote(col_ref, col_ref, sc.at[0, 0], sc.at[1, 0], sibling).wait_send()
+        for which in range(2):
+            col_copy(0, 2, sibling, which).wait_send()
 
     @pl.when(r == own_col)
     def _():
@@ -586,35 +638,39 @@
                 remote(col_p, col_p, sp.at[0, index], sp.at[1, 0], sibling).wait_send()
 
 
-def reduce_and_gather(w, col_part, m_part, heads):
-    f32 = jnp.float32
+def main_call(adjoint, p, q):
+    f32, bf16 = jnp.float32, jnp.bfloat16
     vmem, dma = pltpu.VMEM, pltpu.SemaphoreType.DMA
     here = pl.BlockSpec(memory_space=pltpu.VMEM)
+    there = pl.BlockSpec(memory_space=pl.ANY)
     o, top = pl.pallas_call(
-        reduce_kernel,
+        main_kernel,
         out_shape=(jax.ShapeDtypeStruct((4, 4, 2, 2, 64, 512), f32), jax.ShapeDtypeStruct((NB, 512), f32)),
-        in_specs=[here] * 4,
+        in_specs=[there, there, here],
         out_specs=(here, here),
         scratch_shapes=[
+            vmem((16, NB, 512), f32), vmem((2, 2, NB, NB), f32), vmem((2, HEAD, NB), f32), vmem((2, NB, 512), bf16),
+            vmem((2, NB, 512), bf16), vmem((NB, 512), f32), vmem((4, 4, 2, 2, 64, 512), f32), vmem((2, 2, 128, 512), f32),
+            vmem((2, 4, 128, 512), f32),
             vmem((2, 4, 4, 64, 512), f32), vmem((2, 4, 4, 64, 512), f32), vmem((2, 2, 2, 64, 512), f32), vmem((2, 2, 4, 64, 512), f32),
             vmem((2, 4, 64, 512), f32), vmem((2, 2, 32, 512), f32), vmem((2, 2, 64, 512), f32), vmem((2, NB, NB), f32),
             vmem((3, 2, 2, 128, 512), f32), vmem((128, 512), f32), vmem((4, 128, 512), f32), vmem((4, 128, 512), f32),
             vmem((3, 128, 512), f32), vmem((4, 32, 512), f32), vmem((3, 32, 512), f32), vmem((4, 8, 512), f32), vmem((3, 8, 512), f32),
-            vmem((2, 4, 4, 4, 8, 512), f32),
-            dma((2, 2, 4)), dma((2, 2, 2)), dma((2, 2, 2, 2)), dma((2, 2, 2)), dma((2, 2, 2, 2)), dma((2, 3)), dma((2, 4)),
+            vmem((2, 4, 4, 4, 8, 512), f32), dma((19,)),
+            dma((2, 2, 4)), dma((2, 2, 2)), dma((2, 2, 2, 2)), dma((2, 2, 2)), dma((2, 2, 2, 2)), dma((2, 6)), dma((2, 4)),
             dma((2, 8, 3)), dma((2, 2, 4)), dma((2, 2, 4, 4)), dma((2, 2, 4, 4)),
         ],
-        compiler_params=pltpu.CompilerParams(collective_id=2, has_side_effects=True, vmem_limit_bytes=60 << 20),
-    )(w.reshape(4, 4, 2, 2, 64, 512), col_part.reshape(2, 2, 128, 512), m_part.reshape(2, 4, 128, 512), heads)
+        compiler_params=pltpu.CompilerParams(collective_id=2, has_side_effects=True, vmem_limit_bytes=62 << 20),
+    )(adjoint, p, q)
     return o.reshape(ROWS, 512), top
 
 
 def local(factor, adjoint):
     row_id = lax.axis_index("row")
     p, q = broadcast(factor)
-    w, col_part, m_part = products(adjoint, p, q)
-    out, top = reduce_and_gather(w, col_part, m_part, p[:, ROWS:])
-    return jnp.concatenate([jnp.where(row_id < 2, top, out[:NB]), out[NB:]], 0)
+    out, top = main_call(adjoint, p, q)
+    rows = lax.broadcasted_iota(jnp.int32, out.shape, 0)
+    return jnp.where((rows < NB) & (row_id < 2), jnp.pad(top, ((0, ROWS - NB), (0, 0))), out)
 
 
 def solution(mesh):

time: 217 us -> 184 us (0.85)
  Pallas kernels: 196 us -> 176 us
  local copies, waits for them, and re-layouts: 15.6 us -> 0 us
    pallas_call x2 -> x1, Pallas kernels: 143 us -> 124 us  [main_call(): pl.pallas_call(main_kernel, out_shape=(jax.ShapeDtypeStruct((4, 4, 2, 2,...]
    unnamed x8 -> x0, local copies, waits for them, and re-layouts: 9.09 us -> none
    slice x2 -> x0, local copies, waits for them, and re-layouts: 6.48 us -> none  [the longest x1 4.15 us: local(): return jnp.concatenate([jnp.where(row_id < 2, top, out[:NB]), out[NB:]], 0)]
    select_n x1, other arithmetic: 1.29 us -> 6.11 us  [local(): jnp.where((rows < NB) & (row_id < 2), jnp.pad(top, ((0, ROWS - NB), (0, 0...]
    concatenate x1 -> x0, other arithmetic: 4.38 us -> none  [local(): return jnp.concatenate([jnp.where(row_id < 2, top, out[:NB]), out[NB:]], 0)]
where the time goes in v2:
time: 184 us; the launch traced here: 183 us
  Pallas kernels  176 us (96%)
  other arithmetic  6.12 us (3%)
    pallas_call x1, Pallas kernels, main_call(): pl.pallas_call(main_kernel, out_shape=(jax.ShapeDtypeStruct((4, 4, 2, 2,...  124 us
    pallas_call x1, Pallas kernels, broadcast(): pl.pallas_call(broadcast_kernel, out_shape=(jax.ShapeDtypeStruct((2, ROWS...  52 us
    select_n x1, other arithmetic, local(): jnp.where((rows < NB) & (row_id < 2), jnp.pad(top, ((0, ROWS - NB), (0, 0...  6.11 us

profile of v2, /device:TPU:0, one launch (start us, length us, event | category | flops | bytes accessed | tf_op | source)
XLA Modules:
  0.0 182.6 jit_solution(14179880739318385144)
XLA Ops:
  0.0 52.0 %shard_map.28 = (f32[2,4608,256]{2,1,0:T(8,128)}, f32[2,512,256]{2,1,0:T(8,128)}) custom-call(f32[4096,512]{1,0:T(8,128)} %f_ref.1), custom_call_target="tpu_custom_call" | custom-call | tf_op jit(solution)/shard_map/pallas_call | solution.py:208
  52.0 124.4 %shard_map.29 = (f32[4,4,2,2,64,512]{5,4,3,2,1,0:T(8,128)}, f32[256,512]{1,0:T(8,128)}) custom-call(f32[4096,512]{1,0:T(8,128)} %a_hbm.1, f32[2,4608,256]{2,1,0:T(8,128)} %get-tuple-element.9.p_hbm, f32[2,512,256]{2,1,0:T(8,128)} %get-tuple-element.10.q_ref), custom_call_target="tpu_custom_call" | custom-call | tf_op jit(solution)/shard_map/pallas_call | solution.py:646
  176.5 6.1 %bitcast_select_fusion = f32[4096,512]{1,0:T(8,128)} fusion(f32[4,4,2,2,64,512]{5,4,3,2,1,0:T(8,128)} %get-tuple-element.12, f32[256,512]{1,0:T(8,128)} %get-tuple-element.11, pred[4096]{0:T(1024)(128)(4,1)S(1)} %fusion), kind=kLoop, calls=%fused_computation | loop fusion | flops 2097152 | bytes 17305600 | tf_op jit(solution)/shard_map/jit(_where)/select_n | solution.py:673
  (1 shorter events, 0.0 us)

commit v3 on v2

--- a/solution.py
+++ b/solution.py
@@ -34,7 +34,7 @@
 
 MESH = pl.DeviceIdType.MESH
 ROWS, HEAD, CHUNK = 4096, 512, 32
-STEPS, LAG, AHEAD = 36, 5, 16
+STEPS, LAG, AHEAD = 36, 5, 32
 DEPTH = ((0, 3, 4, 3, 3, 4, 5, 4, 2, 3, 4, 3, 1, 2, 3, 2), (0, 3, 2, 1, 3, 4, 3, 2, 4, 5, 4, 3, 3, 4, 3, 2),
          (0, 3, 4, 3, 1, 2, 3, 2, 2, 3, 4, 3, 3, 4, 5, 4), (0, 1, 2, 3, 3, 2, 3, 4, 4, 3, 4, 5, 3, 2, 3, 4))
 TREE_OF_LINK = ((2, 3, 3, 1, 2, 2, 3, 1, 2, 2, 2, 2, 9, 0, 0, 0), (3, 3, 3, 9, 2, 2, 3, 1, 0, 0, 3, 1, 0, 3, 3, 1),
@@ -95,11 +95,14 @@
         return pl.multiple_of(jnp.where((s >= AHEAD) & (s < AHEAD + 4), head, body), CHUNK)
 
     def pass_on(s, t, src, dst):
+        to_links(s, t, src, dst)
+        remote(src, dst, sib_send.at[s, t], sib_recv.at[s, t], sibling).start()
+
+    def to_links(s, t, src, dst):
         for d in range(4):
             @pl.when(tree[d] == t)
             def _():
                 remote(src, dst, send.at[d, s], recv.at[s, t], nexts[d]).start()
-        remote(src, dst, sib_send.at[s, t], sib_recv.at[s, t], sibling).start()
 
     @pl.when(is_root)
     def _():
@@ -146,7 +149,7 @@
                 pass_on(s, t, rows, rows)
 
     m = c // 4
-    stops = [8 * j + 8 + (4 if 8 * j + 8 > AHEAD else 0) + LAG * 4 for j in range(4)]
+    stops = [8 * j + 8 + (4 if 8 * j >= AHEAD else 0) + LAG * 4 for j in range(4)]
     for j in range(4):
         @pl.when(jnp.logical_not(is_root))
         def _():
@@ -166,6 +169,10 @@
                 pltpu.make_async_copy(src, dst, own.at[2 + j * 2 + b]).start()
                 for i, device in enumerate(xs):
                     remote(src, dst, x_send.at[j, b, i], x_recv.at[j, b], device).start()
+
+    @pl.when(jnp.logical_not(is_root))
+    def _():
+        lax.fori_loop(stops[3], STEPS + LAG * 4, forward, None)
 
     def finish(s, _):
         for t in range(4):

time: 184 us -> 179 us (0.973)
  Pallas kernels: 176 us -> 170 us
    pallas_call x1, Pallas kernels: 124 us -> 121 us  [main_call(): pl.pallas_call(main_kernel, out_shape=(jax.ShapeDtypeStruct((4, 4, 2, 2,...]
    pallas_call x1, Pallas kernels: 52 us -> 49.4 us  [broadcast(): pl.pallas_call(broadcast_kernel, out_shape=(jax.ShapeDtypeStruct((2, ROWS...]
where the time goes in v3:
time: 179 us; the launch traced here: 177 us
  Pallas kernels  170 us (95%)
  other arithmetic  6.12 us (3%)
    pallas_call x1, Pallas kernels, main_call(): pl.pallas_call(main_kernel, out_shape=(jax.ShapeDtypeStruct((4, 4, 2, 2,...  121 us
    pallas_call x1, Pallas kernels, broadcast(): pl.pallas_call(broadcast_kernel, out_shape=(jax.ShapeDtypeStruct((2, ROWS...  49.4 us
    select_n x1, other arithmetic, local(): jnp.where((rows < NB) & (row_id < 2), jnp.pad(top, ((0, ROWS - NB), (0, 0...  6.11 us

profile of v3, /device:TPU:0, one launch (start us, length us, event | category | flops | bytes accessed | tf_op | source)
XLA Modules:
  0.0 176.5 jit_solution(7548022317216407525)
XLA Ops:
  0.0 49.4 %shard_map.28 = (f32[2,4608,256]{2,1,0:T(8,128)}, f32[2,512,256]{2,1,0:T(8,128)}) custom-call(f32[4096,512]{1,0:T(8,128)} %f_ref.1), custom_call_target="tpu_custom_call" | custom-call | tf_op jit(solution)/shard_map/pallas_call | solution.py:215
  49.4 120.9 %shard_map.29 = (f32[4,4,2,2,64,512]{5,4,3,2,1,0:T(8,128)}, f32[256,512]{1,0:T(8,128)}) custom-call(f32[4096,512]{1,0:T(8,128)} %a_hbm.1, f32[2,4608,256]{2,1,0:T(8,128)} %get-tuple-element.9.p_hbm, f32[2,512,256]{2,1,0:T(8,128)} %get-tuple-element.10.q_ref), custom_call_target="tpu_custom_call" | custom-call | tf_op jit(solution)/shard_map/pallas_call | solution.py:653
  170.4 6.1 %bitcast_select_fusion = f32[4096,512]{1,0:T(8,128)} fusion(f32[4,4,2,2,64,512]{5,4,3,2,1,0:T(8,128)} %get-tuple-element.12, f32[256,512]{1,0:T(8,128)} %get-tuple-element.11, pred[4096]{0:T(1024)(128)(4,1)S(1)} %fusion), kind=kLoop, calls=%fused_computation | loop fusion | flops 2097152 | bytes 17305600 | tf_op jit(solution)/shard_map/jit(_where)/select_n | solution.py:680
  (1 shorter events, 0.0 us)
